TPU v7x, 32 devices: a whole 2x2x4 slice. The times are simulated.
32 devices in a mesh: pts: 2 (over core), cen: 16 (over z, y, x).
Axes of the slice: x: 2, y: 2, z: 4, core: 2. Of those that a mesh axis runs over, the one named last changes fastest.
Arguments:
- points: bfloat16 [2, 1024, 256], P(None, ('pts', 'cen')), may hold values from -4096 to 4096, as said below
- centroids: float32 [16384, 256], P('cen'), may hold values from -6 to 6, as said below
Outputs:
- new_centroids: float32 [16384, 256], P('cen')
- energy: float32 [2, 1024], P(None, 'pts')
Inputs may be any that keep to these rules, and one draw needn't show every extreme that they name: Real-valued points. Real-valued centroids.
All inputs are finite; a program needn't handle non-finite values.
Results may differ from a plain program's by a relative error of at most 0.0003.
The roundings to bfloat16 on the way count: a program that leaves them out, or rounds other values in their place, can miss the bound.
Values may be sent and summed in bfloat16 or wider, within the bound.
A program may use at most 64 MiB of HBM per device.

v0:
```python
import functools

import jax
import jax.numpy as jnp
from jax import lax
from jax.experimental import pallas as pl
from jax.experimental.pallas import tpu as pltpu
from jax.sharding import PartitionSpec as P

TEMPER = 32.0
MESH = pl.DeviceIdType.MESH
LANES = 128
ROWS = 256


def split(n):
    near = 1
    while near * near * 4 <= n:
        near *= 2
    assert n % near == 0 and (n // near) & (n // near - 1) == 0
    return n // near, near


def flip(i, d):
    bit = 1
    while bit <= d:
        if d & bit:
            i = i + bit - 2 * bit * lax.rem(i // bit, 2)
        bit *= 2
    return i


def kernel(far, near, n_pts, pts_ref, cen_ref, out_ref, en_ref,
           x_ref, w_ref, cur_ref, low_ref, sq_ref, stat, got,
           z_send, q_send, p_recv, s_send, s_recv, c_send, c_recv,
           in_sem, cen_sem):
    steps, own, dim = pts_ref.shape
    k_loc = cen_ref.shape[0]
    n_blk = k_loc // ROWS
    width = near * own
    cols = width // LANES
    groups = far * cols
    cen = lax.axis_index("cen")
    p = lax.axis_index("pts")
    a = cen // near
    b = lax.rem(cen, near)
    far_peers = [flip(a, d) for d in range(1, far)]
    near_peers = [flip(b, d) for d in range(1, near)]
    pts_peers = [lax.rem(p + d, n_pts) for d in range(1, n_pts)]

    barrier = pltpu.get_barrier_semaphore()
    for peer in far_peers:
        pl.semaphore_signal(barrier, inc=1, device_id={"cen": peer * near + b}, device_id_type=MESH)
    for peer in near_peers:
        pl.semaphore_signal(barrier, inc=1, device_id={"cen": a * near + peer}, device_id_type=MESH)
    for peer in pts_peers:
        pl.semaphore_signal(barrier, inc=1, device_id={"pts": peer}, device_id_type=MESH)

    def lowered(value):
        low = value.astype(jnp.bfloat16).astype(jnp.float32) * (2.0 / TEMPER)
        sq = jnp.sum(value * value, axis=1, keepdims=True) * (1.0 / TEMPER)
        return low.astype(jnp.bfloat16), sq

    def cen_copy(blk):
        rows = pl.ds(pl.multiple_of(blk * ROWS, ROWS), ROWS)
        return pltpu.make_async_copy(cen_ref.at[rows, :], cur_ref.at[rows, :], cen_sem.at[blk])

    def pts_copy(s):
        return pltpu.make_async_copy(pts_ref.at[s], x_ref.at[s, a, pl.ds(b * own, own), :], in_sem.at[s])

    for s in range(steps):
        pts_copy(s).start()

    @pl.loop(0, n_blk)
    def _(blk):
        cen_copy(blk).start()

    for s in range(steps):
        pts_copy(s).wait()

    @pl.loop(0, n_blk)
    def _(blk):
        cen_copy(blk).wait()
        rows = pl.ds(pl.multiple_of(blk * ROWS, ROWS), ROWS)
        low_ref[rows, :], sq = lowered(cur_ref[rows, :])
        sq_ref[rows, :] = jnp.broadcast_to(sq, (ROWS, LANES))

    pl.semaphore_wait(barrier, len(far_peers) + len(near_peers) + len(pts_peers))

    def chunk(s, i, j):
        return x_ref.at[s, i, pl.ds(j * own, own), :]

    def far_copy(s, d):
        peer = flip(a, d)
        return pltpu.make_async_remote_copy(
            src_ref=chunk(s, a, b), dst_ref=chunk(s, a, b),
            send_sem=z_send.at[s, d], recv_sem=p_recv.at[s, a, b],
            device_id={"cen": peer * near + b}, device_id_type=MESH)

    def near_copy(s, i, d):
        peer = flip(b, d)
        return pltpu.make_async_remote_copy(
            src_ref=chunk(s, i, b), dst_ref=chunk(s, i, b),
            send_sem=q_send.at[s, i, d], recv_sem=p_recv.at[s, i, b],
            device_id={"cen": a * near + peer}, device_id_type=MESH)

    def own_near_copy(s, d):
        peer = flip(b, d)
        return pltpu.make_async_remote_copy(
            src_ref=chunk(s, a, b), dst_ref=chunk(s, a, b),
            send_sem=q_send.at[s, a, d], recv_sem=p_recv.at[s, a, b],
            device_id={"cen": a * near + peer}, device_id_type=MESH)

    def arrived(s, i, j):
        pltpu.make_async_remote_copy(
            src_ref=chunk(s, i, j), dst_ref=chunk(s, i, j),
            send_sem=z_send.at[s, 0], recv_sem=p_recv.at[s, i, j],
            device_id={"cen": cen}, device_id_type=MESH).wait_recv()

    def send_own(s):
        for d in reversed(range(1, far)):
            far_copy(s, d).start()
        for d in reversed(range(1, near)):
            own_near_copy(s, d).start()

    def forward(s):
        for d in range(1, far):
            i = flip(a, d)
            arrived(s, i, b)
            for e in reversed(range(1, near)):
                near_copy(s, i, e).start()

    def stat_copy(s, d):
        return pltpu.make_async_remote_copy(
            src_ref=stat.at[s, cen], dst_ref=stat.at[s, cen],
            send_sem=s_send.at[s, d], recv_sem=s_recv.at[s, cen],
            device_id={"cen": flip(cen, d)}, device_id_type=MESH)

    def sums_copy(s, d, blk):
        peer = lax.rem(p + d, n_pts)
        return pltpu.make_async_remote_copy(
            src_ref=got.at[s, p, blk], dst_ref=got.at[s, p, blk],
            send_sem=c_send.at[s, d, blk], recv_sem=c_recv.at[s, p, blk],
            device_id={"pts": peer}, device_id_type=MESH)

    def landed(ref, sem):
        pltpu.make_async_remote_copy(
            src_ref=ref, dst_ref=ref, send_sem=z_send.at[0, 0], recv_sem=sem,
            device_id={"cen": cen}, device_id_type=MESH).wait_recv()

    def joined(s):
        tops = stat[s, :, 0]
        top = jnp.max(tops, axis=0)
        return top, jnp.sum(stat[s, :, 1] * jnp.exp(tops - top[None]), axis=0)

    send_own(0)
    forward(0)
    send_own(1) if steps > 1 else None

    for s in range(steps):
        def one_group(i):
            for e in range(1, near):
                arrived(s, i, flip(b, e))
            for j in range(cols):
                xg = x_ref[s, i, j * LANES:(j + 1) * LANES, :]
                logits = lax.dot_general(
                    low_ref[...], xg, (((1,), (1,)), ((), ())),
                    preferred_element_type=jnp.float32) - sq_ref[...]
                top = jnp.max(logits, axis=0, keepdims=True)
                weights = jnp.exp(logits - top)
                g = i * cols + j
                w_ref[:, pl.ds(pl.multiple_of(g * LANES, LANES), LANES)] = weights
                stat[s, cen, 0, pl.ds(g, 1), :] = top
                stat[s, cen, 1, pl.ds(g, 1), :] = jnp.sum(weights, axis=0, keepdims=True)

        if s == 0:
            for d in range(far):
                one_group(flip(a, d))
        for d in reversed(range(1, far * near)):
            stat_copy(s, d).start()
        if s + 1 < steps:
            forward(s + 1)
            if s + 2 < steps:
                send_own(s + 2)
        for d in range(1, far * near):
            i = flip(cen, d)
            landed(stat.at[s, i], s_recv.at[s, i])
        top, total = joined(s)
        energy = top + jnp.log(total)
        scale = jnp.exp(stat[s, cen, 0] - top) / total
        for g in range(groups):
            en_ref[s:s + 1, g * LANES:(g + 1) * LANES] = energy[g:g + 1, :]
        scale = jnp.concatenate([scale[g:g + 1, :] for g in range(groups)], axis=1)

        @pl.loop(0, n_blk)
        def _(blk):
            rows = pl.ds(pl.multiple_of(blk * ROWS, ROWS), ROWS)
            resp = w_ref[rows, :] * scale
            part = resp[:, :LANES]
            for g in range(1, groups):
                part = part + resp[:, g * LANES:(g + 1) * LANES]
            count = jnp.sum(jnp.transpose(part), axis=0, keepdims=True)
            xs = x_ref[s].reshape(far * width, dim)
            sums = lax.dot_general(
                resp.astype(jnp.bfloat16), xs, (((1,), (0,)), ((), ())),
                preferred_element_type=jnp.float32)
            got[s, p, blk, :ROWS, :] = sums
            got[s, p, blk, ROWS:ROWS + 1, :] = count
            for d in range(1, n_pts):
                sums_copy(s, d, blk).start()

        if s + 1 < steps:
            for d in range(far):
                for e in range(1, near):
                    arrived(s + 1, flip(a, d), flip(b, e))

        def finish(blk, top):
            rows = pl.ds(pl.multiple_of(blk * ROWS, ROWS), ROWS)
            for d in range(1, n_pts):
                i = lax.rem(p + d, n_pts)
                landed(got.at[s, i, blk], c_recv.at[s, i, blk])
            sums = got[s, 0, blk, :ROWS, :]
            count = got[s, 0, blk, ROWS:ROWS + 1, :]
            for i in range(1, n_pts):
                sums = sums + got[s, i, blk, :ROWS, :]
                count = count + got[s, i, blk, ROWS:ROWS + 1, :]
            column = jnp.transpose(jnp.broadcast_to(1.0 + count, (LANES, ROWS)))
            column = jnp.concatenate([column] * (dim // LANES), axis=1)
            value = (cur_ref[rows, :] + sums) / column
            if s + 1 == steps:
                out_ref[rows, :] = value
                return top
            cur_ref[rows, :] = value
            low, sq = lowered(value)
            logits = lax.dot_general(
                low, x_ref[s + 1].reshape(far * width, dim), (((1,), (1,)), ((), ())),
                preferred_element_type=jnp.float32) - sq
            w_ref[rows, :] = logits
            return jnp.maximum(top, jnp.max(logits, axis=0, keepdims=True))

        def weigh(top, blk, total):
            rows = pl.ds(pl.multiple_of(blk * ROWS, ROWS), ROWS)
            weights = jnp.exp(w_ref[rows, :] - top)
            w_ref[rows, :] = weights
            return total + jnp.sum(weights, axis=0, keepdims=True)

        top = lax.fori_loop(0, n_blk, finish, jnp.full((1, groups * LANES), -jnp.inf, jnp.float32))
        if s + 1 < steps:
            total = lax.fori_loop(0, n_blk, functools.partial(weigh, top), jnp.zeros_like(top))
            for g in range(groups):
                stat[s + 1, cen, 0, g:g + 1, :] = top[:, g * LANES:(g + 1) * LANES]
                stat[s + 1, cen, 1, g:g + 1, :] = total[:, g * LANES:(g + 1) * LANES]

    for s in range(steps):
        for d in range(1, far * near):
            stat_copy(s, d).wait_send()
        for d in range(1, far):
            far_copy(s, d).wait_send()
            for e in range(1, near):
                near_copy(s, flip(a, d), e).wait_send()
        for d in range(1, near):
            own_near_copy(s, d).wait_send()

        @pl.loop(0, n_blk)
        def _(blk):
            for d in range(1, n_pts):
                sums_copy(s, d, blk).wait_send()


def on_device(far, near, n_pts, points, centroids):
    steps, own, dim = points.shape
    k_loc = centroids.shape[0]
    n_blk = k_loc // ROWS
    batch = far * near * own
    groups = batch // LANES
    vmem = pl.BlockSpec(memory_space=pltpu.VMEM)
    dma = pltpu.SemaphoreType.DMA
    return pl.pallas_call(
        functools.partial(kernel, far, near, n_pts),
        out_shape=(pltpu.VMEM((k_loc, dim), jnp.float32),
                   pltpu.VMEM((steps, batch), jnp.float32)),
        in_specs=[pl.BlockSpec(memory_space=pl.ANY)] * 2,
        out_specs=(vmem, vmem),
        scratch_shapes=[
            pltpu.VMEM((steps, far, near * own, dim), jnp.bfloat16),
            pltpu.VMEM((k_loc, batch), jnp.float32),
            pltpu.VMEM((k_loc, dim), jnp.float32),
            pltpu.VMEM((k_loc, dim), jnp.bfloat16),
            pltpu.VMEM((k_loc, LANES), jnp.float32),
            pltpu.VMEM((steps, far * near, 2, groups, LANES), jnp.float32),
            pltpu.VMEM((steps, n_pts, n_blk, ROWS + 8, dim), jnp.float32),
            dma((steps, far)),
            dma((steps, far, near)),
            dma((steps, far, near)),
            dma((steps, far * near)),
            dma((steps, far * near)),
            dma((steps, n_pts, n_blk)),
            dma((steps, n_pts, n_blk)),
            dma((steps,)),
            dma((n_blk,)),
        ],
        compiler_params=pltpu.CompilerParams(
            collective_id=0, has_side_effects=True, vmem_limit_bytes=60 * 1024 * 1024),
    )(points, centroids)


def solution(mesh):
    far, near = split(mesh.shape["cen"])
    placed = (P(None, ("pts", "cen"), None), P("cen", None))
    return jax.shard_map(
        functools.partial(on_device, far, near, mesh.shape["pts"]),
        mesh=mesh,
        in_specs=placed,
        out_specs=(P("cen", None), P(None, "pts")),
        check_vma=False,
    )
```

profile of v0, /device:TPU:0, one launch (start us, length us, event | category | flops | bytes accessed | tf_op | source)
XLA Modules:
  0.0 32.1 jit_solution(13420432417532691248)
XLA Ops:
  0.6 29.9 %shard_map.41 = (f32[1024,256]{1,0:T(8,128)S(1)}, f32[2,512]{1,0:T(2,128)S(1)}) custom-call(bf16[2,32,256]{2,1,0:T(8,128)(2,1)} %pts_ref.1, f32[1024,256]{1,0:T(8,128)} %cen_ref.1), custom_call_target="tpu_custom_call" | custom-call | tf_op jit(solution)/shard_map/pallas_call | solution.py:278
  30.6 1.0 %copy.6 = f32[1024,256]{1,0:T(8,128)} copy(f32[1024,256]{1,0:T(8,128)S(1)} %get-tuple-element.2) | data formatting | bytes 2097152
  31.5 0.6 %copy.7 = f32[2,512]{1,0:T(2,128)} copy(f32[2,512]{1,0:T(2,128)S(1)} %get-tuple-element.3) | data formatting | bytes 8192
where the time goes:
time: 32.4 us; the launch traced here: 32.1 us
  Pallas kernels  29.9 us (92%)
  local copies, waits for them, and re-layouts  1.56 us (5%)
  between operations  0.64 us (2%)
    pallas_call x1, Pallas kernels, on_device(): pl.pallas_call(functools.partial(kernel, far, near, n_pts), out_shape=(pl...  29.9 us
    unnamed x2, local copies, waits for them, and re-layouts  1.56 us

commit v1 on v0

v1 whole, which is shorter than its diff:
```python
import functools

import jax
import jax.numpy as jnp
from jax import lax
from jax.experimental import pallas as pl
from jax.experimental.pallas import tpu as pltpu
from jax.sharding import PartitionSpec as P

TEMPER = 32.0
MESH = pl.DeviceIdType.MESH
LANES = 128
ROWS = 256


def split(n):
    near = 1
    while near * near * 4 <= n:
        near *= 2
    assert n % near == 0 and (n // near) & (n // near - 1) == 0
    return n // near, near


def flips(i, n):
    steps, bit = [], 1
    while bit < n:
        steps.append((bit, bit - 2 * bit * lax.rem(i // bit, 2)))
        bit *= 2
    peers = []
    for d in range(n):
        peer = i
        for bit, step in steps:
            if d & bit:
                peer = peer + step
        peers.append(peer)
    return peers


def kernel(far, near, n_pts, pts_ref, cen_ref, out_ref, en_ref,
           x_ref, w_ref, cur_ref, low_ref, sq_ref, tops, stat, got,
           p_send, f_recv, n_recv, s_send, s_recv, c_send, c_recv,
           in_sem, cen_sem):
    steps, own, dim = pts_ref.shape
    k_loc = cen_ref.shape[0]
    n_blk = k_loc // ROWS
    n_cen = far * near
    width = near * own
    cols = width // LANES
    groups = far * cols
    cen = lax.axis_index("cen")
    p = lax.axis_index("pts")
    a = cen // near
    b = lax.rem(cen, near)
    a_flip = flips(a, far)
    b_flip = flips(b, near)
    pts_peers = [lax.rem(p + d, n_pts) for d in range(1, n_pts)]

    barrier = pltpu.get_barrier_semaphore()
    for peer in a_flip[1:]:
        pl.semaphore_signal(barrier, inc=1, device_id={"cen": peer * near + b}, device_id_type=MESH)
    for peer in b_flip[1:]:
        pl.semaphore_signal(barrier, inc=1, device_id={"cen": a * near + peer}, device_id_type=MESH)
    for peer in pts_peers:
        pl.semaphore_signal(barrier, inc=1, device_id={"pts": peer}, device_id_type=MESH)

    def rows_of(blk):
        return pl.ds(pl.multiple_of(blk * ROWS, ROWS), ROWS)

    def lowered(value):
        sq = jnp.sum(value * value, axis=1, keepdims=True) * (1.0 / TEMPER)
        return (value * (2.0 / TEMPER)).astype(jnp.bfloat16), sq

    def cen_copy(blk):
        rows = rows_of(blk)
        return pltpu.make_async_copy(cen_ref.at[rows, :], cur_ref.at[rows, :], cen_sem.at[blk])

    def chunk(s, i, j):
        return x_ref.at[s, pl.ds(pl.multiple_of((i * near + j) * own, own), own), :]

    def pts_copy(s):
        return pltpu.make_async_copy(pts_ref.at[s], chunk(s, a, b), in_sem.at[s])

    def landed(ref, sem):
        pltpu.make_async_remote_copy(
            src_ref=ref, dst_ref=ref, send_sem=sem, recv_sem=sem,
            device_id={"cen": cen}, device_id_type=MESH).wait_recv()

    def sent(ref, sem):
        pltpu.make_async_remote_copy(
            src_ref=ref, dst_ref=ref, send_sem=sem, recv_sem=sem,
            device_id={"cen": cen}, device_id_type=MESH).wait_send()

    def chunks(s, n):
        return x_ref.at[s, pl.ds(0, n * own), :]

    def far_sem(s, i):
        return f_recv.at[i if s == 0 else far + s - 1]

    def near_sem(s, i):
        return n_recv.at[i if s == 0 else far + s - 1]

    def far_copy(s, d):
        return pltpu.make_async_remote_copy(
            src_ref=pts_ref.at[s], dst_ref=chunk(s, a, b),
            send_sem=p_send.at[s], recv_sem=far_sem(s, a),
            device_id={"cen": a_flip[d] * near + b}, device_id_type=MESH)

    def near_copy(s, i, d, src):
        return pltpu.make_async_remote_copy(
            src_ref=src, dst_ref=chunk(s, i, b),
            send_sem=p_send.at[s], recv_sem=near_sem(s, i),
            device_id={"cen": a * near + b_flip[d]}, device_id_type=MESH)

    def send_own(s):
        for d in reversed(range(1, far)):
            far_copy(s, d).start()
        for d in reversed(range(1, near)):
            near_copy(s, a, d, pts_ref.at[s]).start()

    def forward(s):
        if s > 0:
            landed(chunks(s, far - 1), far_sem(s, 0))
        for d in range(1, far):
            i = a_flip[d]
            if s == 0:
                landed(chunk(s, i, b), far_sem(s, i))
            for e in reversed(range(1, near)):
                near_copy(s, i, e, chunk(s, i, b)).start()

    def stat_copy(s, d):
        return pltpu.make_async_remote_copy(
            src_ref=stat.at[s, cen], dst_ref=stat.at[s, cen],
            send_sem=s_send.at[s], recv_sem=s_recv.at[s],
            device_id={"cen": a_flip[d // near] * near + b_flip[d % near]}, device_id_type=MESH)

    def sums_copy(s, d, blk):
        return pltpu.make_async_remote_copy(
            src_ref=got.at[s, p, blk], dst_ref=got.at[s, p, blk],
            send_sem=c_send.at[s], recv_sem=c_recv.at[s, blk],
            device_id={"pts": pts_peers[d - 1]}, device_id_type=MESH)

    for s in range(steps):
        pts_copy(s).start()

    @pl.loop(0, n_blk)
    def _(blk):
        cen_copy(blk).start()

    with jax.named_scope("entry"):
        pl.semaphore_wait(barrier, (far - 1) + (near - 1) + (n_pts - 1))
        send_own(0)

    with jax.named_scope("prepare"):
        @pl.loop(0, n_blk)
        def _(blk):
            cen_copy(blk).wait()
            rows = rows_of(blk)
            low_ref[rows, :], sq = lowered(cur_ref[rows, :])
            sq_ref[rows, :] = jnp.broadcast_to(sq, (ROWS, LANES))

    with jax.named_scope("forward0"):
        forward(0)
    if steps > 1:
        send_own(1)
    for s in range(steps):
        pts_copy(s).wait()

    def one_group(i):
        landed(chunks(0, near - 1), near_sem(0, i))
        for j in range(cols):
            g = i * cols + j
            xg = x_ref[0, pl.ds(pl.multiple_of(g * LANES, LANES), LANES), :]
            logits = lax.dot_general(
                low_ref[...], xg, (((1,), (1,)), ((), ())),
                preferred_element_type=jnp.float32) - sq_ref[...]
            top = jnp.max(logits, axis=0, keepdims=True)
            weights = jnp.exp(logits - top)
            w_ref[:, pl.ds(pl.multiple_of(g * LANES, LANES), LANES)] = weights
            tops[pl.ds(g, 1), :] = top
            stat[0, cen, pl.ds(g, 1), :] = top + jnp.log(jnp.sum(weights, axis=0, keepdims=True))

    for d in range(far):
        with jax.named_scope("group" + str(d)):
            one_group(a_flip[d])

    for s in range(steps):
        for d in reversed(range(1, n_cen)):
            stat_copy(s, d).start()
        if s + 1 < steps:
            with jax.named_scope("forward1"):
                forward(s + 1)
            if s + 2 < steps:
                send_own(s + 2)
        with jax.named_scope("stats" + str(s)):
            landed(stat.at[s, pl.ds(0, n_cen - 1)], s_recv.at[s])
        parts = stat[s]
        best = jnp.max(parts, axis=0)
        energy = best + jnp.log(jnp.sum(jnp.exp(parts - best[None]), axis=0))
        scale = jnp.exp(tops[...] - energy)
        for g in range(groups):
            en_ref[s:s + 1, g * LANES:(g + 1) * LANES] = energy[g:g + 1, :]
        scale = jnp.concatenate([scale[g:g + 1, :] for g in range(groups)], axis=1)

        with jax.named_scope("sums" + str(s)):
            @pl.loop(0, n_blk)
            def _(blk):
                resp = w_ref[rows_of(blk), :] * scale
                part = resp[:, :LANES]
                for g in range(1, groups):
                    part = part + resp[:, g * LANES:(g + 1) * LANES]
                count = jnp.sum(jnp.transpose(part), axis=0, keepdims=True)
                sums = lax.dot_general(
                    resp.astype(jnp.bfloat16), x_ref[s], (((1,), (0,)), ((), ())),
                    preferred_element_type=jnp.float32)
                got[s, p, blk, :ROWS, :] = sums
                got[s, p, blk, ROWS:ROWS + 1, :] = count
                for d in range(1, n_pts):
                    sums_copy(s, d, blk).start()

        if s + 1 < steps:
            landed(chunks(s + 1, far * (near - 1)), near_sem(s + 1, 0))

        def finish(blk, top):
            rows = rows_of(blk)
            landed(got.at[s, pl.ds(0, n_pts - 1), blk], c_recv.at[s, blk])
            sums = got[s, 0, blk, :ROWS, :]
            count = got[s, 0, blk, ROWS:ROWS + 1, :]
            for i in range(1, n_pts):
                sums = sums + got[s, i, blk, :ROWS, :]
                count = count + got[s, i, blk, ROWS:ROWS + 1, :]
            column = jnp.transpose(jnp.broadcast_to(1.0 / (1.0 + count), (LANES, ROWS)))
            column = jnp.concatenate([column] * (dim // LANES), axis=1)
            value = (cur_ref[rows, :] + sums) * column
            if s + 1 == steps:
                out_ref[rows, :] = value
                return top
            cur_ref[rows, :] = value
            low, sq = lowered(value)
            logits = lax.dot_general(
                low, x_ref[s + 1], (((1,), (1,)), ((), ())),
                preferred_element_type=jnp.float32) - sq
            w_ref[rows, :] = logits
            return jnp.maximum(top, jnp.max(logits, axis=0, keepdims=True))

        def weigh(top, blk, total):
            rows = rows_of(blk)
            weights = jnp.exp(w_ref[rows, :] - top)
            w_ref[rows, :] = weights
            return total + jnp.sum(weights, axis=0, keepdims=True)

        with jax.named_scope("finish" + str(s)):
            top = lax.fori_loop(0, n_blk, finish, jnp.full((1, groups * LANES), -jnp.inf, jnp.float32))
        if s + 1 < steps:
            with jax.named_scope("weigh"):
                total = lax.fori_loop(0, n_blk, functools.partial(weigh, top), jnp.zeros_like(top))
            part = top + jnp.log(total)
            for g in range(groups):
                tops[g:g + 1, :] = top[:, g * LANES:(g + 1) * LANES]
                stat[s + 1, cen, g:g + 1, :] = part[:, g * LANES:(g + 1) * LANES]

    with jax.named_scope("drain"):
        for s in range(steps):
            sent(chunks(s, n_cen - 1), p_send.at[s])
            sent(stat.at[s, pl.ds(0, n_cen - 1)], s_send.at[s])
            sent(got.at[s, pl.ds(0, n_pts - 1)], c_send.at[s])


def emit(value_ref, part_ref, out_ref, en_ref, sems):
    copies = [pltpu.make_async_copy(value_ref, out_ref, sems.at[0]),
              pltpu.make_async_copy(part_ref, en_ref, sems.at[1])]
    for copy in copies:
        copy.start()
    for copy in copies:
        copy.wait()


def on_device(far, near, n_pts, points, centroids):
    steps, own, dim = points.shape
    k_loc = centroids.shape[0]
    n_blk = k_loc // ROWS
    n_cen = far * near
    batch = n_cen * own
    groups = batch // LANES
    vmem = pl.BlockSpec(memory_space=pltpu.VMEM)
    dma = pltpu.SemaphoreType.DMA
    value, energy = pl.pallas_call(
        functools.partial(kernel, far, near, n_pts),
        out_shape=(pltpu.VMEM((k_loc, dim), jnp.float32),
                   pltpu.VMEM((steps, batch), jnp.float32)),
        in_specs=[pl.BlockSpec(memory_space=pl.ANY)] * 2,
        out_specs=(vmem, vmem),
        scratch_shapes=[
            pltpu.VMEM((steps, batch, dim), jnp.bfloat16),
            pltpu.VMEM((k_loc, batch), jnp.float32),
            pltpu.VMEM((k_loc, dim), jnp.float32),
            pltpu.VMEM((k_loc, dim), jnp.bfloat16),
            pltpu.VMEM((k_loc, LANES), jnp.float32),
            pltpu.VMEM((groups, LANES), jnp.float32),
            pltpu.VMEM((steps, n_cen, groups, LANES), jnp.float32),
            pltpu.VMEM((steps, n_pts, n_blk, ROWS + 8, dim), jnp.float32),
            dma((steps,)),
            dma((far + steps - 1,)),
            dma((far + steps - 1,)),
            dma((steps,)),
            dma((steps,)),
            dma((steps,)),
            dma((steps, n_blk)),
            dma((steps,)),
            dma((n_blk,)),
        ],
        compiler_params=pltpu.CompilerParams(
            collective_id=0, has_side_effects=True, vmem_limit_bytes=58 * 1024 * 1024),
    )(points, centroids)
    return pl.pallas_call(
        emit,
        out_shape=(jax.ShapeDtypeStruct((k_loc, dim), jnp.float32),
                   jax.ShapeDtypeStruct((steps, batch), jnp.float32)),
        in_specs=[vmem, vmem],
        out_specs=[pl.BlockSpec(memory_space=pltpu.HBM)] * 2,
        scratch_shapes=[dma((2,))],
        compiler_params=pltpu.CompilerParams(vmem_limit_bytes=1024 * 1024),
    )(value, energy)


def solution(mesh):
    far, near = split(mesh.shape["cen"])
    placed = (P(None, ("pts", "cen"), None), P("cen", None))
    return jax.shard_map(
        functools.partial(on_device, far, near, mesh.shape["pts"]),
        mesh=mesh,
        in_specs=placed,
        out_specs=(P("cen", None), P(None, "pts")),
        check_vma=False,
    )
```

time: 32.4 us -> 30.4 us (0.938)
  local copies, waits for them, and re-layouts: 1.56 us -> 0 us
    unnamed x2 -> x0, local copies, waits for them, and re-layouts: 1.56 us -> none
    pallas_call x1, Pallas kernels: 29.9 us -> 28.6 us  [on_device(): pl.pallas_call(functools.partial(kernel, far, near, n_pts), out_shape=(pl...]
    pallas_call x0 -> x1, Pallas kernels: none -> 0.99 us  [on_device(): pl.pallas_call(emit, out_shape=(jax.ShapeDtypeStruct((k_loc, dim), jnp.fl...]
where the time goes in v1:
time: 30.4 us; the launch traced here: 30.2 us
  Pallas kernels  29.6 us (97%)
  between operations  0.64 us (2%)
    pallas_call x1, Pallas kernels, on_device(): pl.pallas_call(functools.partial(kernel, far, near, n_pts), out_shape=(pl...  28.6 us
    pallas_call x1, Pallas kernels, on_device(): pl.pallas_call(emit, out_shape=(jax.ShapeDtypeStruct((k_loc, dim), jnp.fl...  0.99 us

profile of v1, /device:TPU:0, one launch (start us, length us, event | category | flops | bytes accessed | tf_op | source)
XLA Modules:
  0.0 30.2 jit_solution(8629604952461653351)
XLA Ops:
  0.6 28.6 %shard_map.41 = (f32[1024,256]{1,0:T(8,128)S(1)}, f32[2,512]{1,0:T(2,128)S(1)}) custom-call(bf16[2,32,256]{2,1,0:T(8,128)(2,1)} %pts_ref.1, f32[1024,256]{1,0:T(8,128)} %cen_ref.1), custom_call_target="tpu_custom_call" | custom-call | tf_op jit(solution)/shard_map/pallas_call | solution.py:286
  29.2 1.0 %shard_map.42 = (f32[1024,256]{1,0:T(8,128)}, f32[2,512]{1,0:T(2,128)}) custom-call(f32[1024,256]{1,0:T(8,128)S(1)} %get-tuple-element.4.value_ref, f32[2,512]{1,0:T(2,128)S(1)} %get-tuple-element.5.part_ref), custom_call_target="tpu_custom_call" | custom-call | tf_op jit(solution)/shard_map/pallas_call | solution.py:314

commit v2 on v1

--- a/solution.py
+++ b/solution.py
@@ -11,6 +11,8 @@
 MESH = pl.DeviceIdType.MESH
 LANES = 128
 ROWS = 256
+BLOCK = 128
+UNROLL = 32
 
 
 def split(n):
@@ -37,7 +39,7 @@
 
 
 def kernel(far, near, n_pts, pts_ref, cen_ref, out_ref, en_ref,
-           x_ref, w_ref, cur_ref, low_ref, sq_ref, tops, stat, got,
+           x_ref, w_ref, cur_ref, low_ref, sq_ref, block_top, whole, stat, got,
            p_send, f_recv, n_recv, s_send, s_recv, c_send, c_recv,
            in_sem, cen_sem):
     steps, own, dim = pts_ref.shape
@@ -47,6 +49,7 @@
     width = near * own
     cols = width // LANES
     groups = far * cols
+    unroll = groups * n_blk <= UNROLL
     cen = lax.axis_index("cen")
     p = lax.axis_index("pts")
     a = cen // near
@@ -64,7 +67,21 @@
         pl.semaphore_signal(barrier, inc=1, device_id={"pts": peer}, device_id_type=MESH)
 
     def rows_of(blk):
-        return pl.ds(pl.multiple_of(blk * ROWS, ROWS), ROWS)
+        return pl.ds(blk * ROWS if isinstance(blk, int) else pl.multiple_of(blk * ROWS, ROWS), ROWS)
+
+    def each(body):
+        if unroll:
+            for blk in range(n_blk):
+                body(blk)
+        else:
+            pl.loop(0, n_blk)(body)
+
+    def folded(body, value):
+        if unroll:
+            for blk in range(n_blk):
+                value = body(blk, value)
+            return value
+        return lax.fori_loop(0, n_blk, body, value)
 
     def lowered(value):
         sq = jnp.sum(value * value, axis=1, keepdims=True) * (1.0 / TEMPER)
@@ -74,11 +91,11 @@
         rows = rows_of(blk)
         return pltpu.make_async_copy(cen_ref.at[rows, :], cur_ref.at[rows, :], cen_sem.at[blk])
 
-    def chunk(s, i, j):
-        return x_ref.at[s, pl.ds(pl.multiple_of((i * near + j) * own, own), own), :]
+    def chunk(s, d):
+        return x_ref.at[s, pl.ds(pl.multiple_of(d * width + b * own, own), own), :]
 
     def pts_copy(s):
-        return pltpu.make_async_copy(pts_ref.at[s], chunk(s, a, b), in_sem.at[s])
+        return pltpu.make_async_copy(pts_ref.at[s], chunk(s, 0), in_sem.at[s])
 
     def landed(ref, sem):
         pltpu.make_async_remote_copy(
@@ -93,39 +110,34 @@
     def chunks(s, n):
         return x_ref.at[s, pl.ds(0, n * own), :]
 
-    def far_sem(s, i):
-        return f_recv.at[i if s == 0 else far + s - 1]
-
-    def near_sem(s, i):
-        return n_recv.at[i if s == 0 else far + s - 1]
-
     def far_copy(s, d):
         return pltpu.make_async_remote_copy(
-            src_ref=pts_ref.at[s], dst_ref=chunk(s, a, b),
-            send_sem=p_send.at[s], recv_sem=far_sem(s, a),
+            src_ref=pts_ref.at[s], dst_ref=chunk(s, d),
+            send_sem=p_send.at[s], recv_sem=f_recv.at[d if s == 0 else far + s - 1],
             device_id={"cen": a_flip[d] * near + b}, device_id_type=MESH)
 
-    def near_copy(s, i, d, src):
+    def near_copy(s, d, e):
         return pltpu.make_async_remote_copy(
-            src_ref=src, dst_ref=chunk(s, i, b),
-            send_sem=p_send.at[s], recv_sem=near_sem(s, i),
-            device_id={"cen": a * near + b_flip[d]}, device_id_type=MESH)
-
-    def send_own(s):
+            src_ref=pts_ref.at[s] if d == 0 else chunk(s, d), dst_ref=chunk(s, d),
+            send_sem=p_send.at[s], recv_sem=n_recv.at[min(d, 1) if s == 0 else s + 1],
+            device_id={"cen": a * near + b_flip[e]}, device_id_type=MESH)
+
+    def send_near(s, d):
+        for e in reversed(range(1, near)):
+            near_copy(s, d, e).start()
+
+    def send_far(s):
         for d in reversed(range(1, far)):
             far_copy(s, d).start()
-        for d in reversed(range(1, near)):
-            near_copy(s, a, d, pts_ref.at[s]).start()
 
     def forward(s):
         if s > 0:
-            landed(chunks(s, far - 1), far_sem(s, 0))
+            send_near(s, 0)
+            landed(chunks(s, far - 1), f_recv.at[far + s - 1])
         for d in range(1, far):
-            i = a_flip[d]
             if s == 0:
-                landed(chunk(s, i, b), far_sem(s, i))
-            for e in reversed(range(1, near)):
-                near_copy(s, i, e, chunk(s, i, b)).start()
+                landed(chunk(s, d), f_recv.at[d])
+            send_near(s, d)
 
     def stat_copy(s, d):
         return pltpu.make_async_remote_copy(
@@ -148,7 +160,8 @@
 
     with jax.named_scope("entry"):
         pl.semaphore_wait(barrier, (far - 1) + (near - 1) + (n_pts - 1))
-        send_own(0)
+        send_far(0)
+        send_near(0, 0)
 
     with jax.named_scope("prepare"):
         @pl.loop(0, n_blk)
@@ -161,27 +174,46 @@
     with jax.named_scope("forward0"):
         forward(0)
     if steps > 1:
-        send_own(1)
+        send_far(1)
     for s in range(steps):
         pts_copy(s).wait()
 
-    def one_group(i):
-        landed(chunks(0, near - 1), near_sem(0, i))
+    def combine(pairs):
+        best = functools.reduce(jnp.maximum, [top for top, _ in pairs])
+        return best, sum(jnp.exp(top - best) * total for top, total in pairs)
+
+    def keep(s, d, top, total):
+        part = top + jnp.log(total)
         for j in range(cols):
-            g = i * cols + j
-            xg = x_ref[0, pl.ds(pl.multiple_of(g * LANES, LANES), LANES), :]
+            lanes = slice(j * LANES, (j + 1) * LANES)
+            stat[s, cen, pl.ds(a_flip[d] * cols + j, 1), :] = part[:, lanes]
+
+    def weights_of(d, n, size):
+        xs = x_ref[0, d * width:(d + n) * width, :]
+        pairs = []
+        for k in range(0, k_loc, size):
+            rows = slice(k, k + size)
             logits = lax.dot_general(
-                low_ref[...], xg, (((1,), (1,)), ((), ())),
-                preferred_element_type=jnp.float32) - sq_ref[...]
+                low_ref[rows, :], xs, (((1,), (1,)), ((), ())),
+                preferred_element_type=jnp.float32)
+            logits = logits - jnp.concatenate([sq_ref[rows, :]] * (n * cols), axis=1)
             top = jnp.max(logits, axis=0, keepdims=True)
             weights = jnp.exp(logits - top)
-            w_ref[:, pl.ds(pl.multiple_of(g * LANES, LANES), LANES)] = weights
-            tops[pl.ds(g, 1), :] = top
-            stat[0, cen, pl.ds(g, 1), :] = top + jnp.log(jnp.sum(weights, axis=0, keepdims=True))
-
-    for d in range(far):
-        with jax.named_scope("group" + str(d)):
-            one_group(a_flip[d])
+            w_ref[rows, d * width:(d + n) * width] = weights
+            block_top[k // size, 0:1, d * width:(d + n) * width] = top
+            pairs.append((top, jnp.sum(weights, axis=0, keepdims=True)))
+        top, total = combine(pairs)
+        for i in range(n):
+            lanes = slice(i * width, (i + 1) * width)
+            keep(0, d + i, top[:, lanes], total[:, lanes])
+
+    with jax.named_scope("group0"):
+        landed(chunks(0, near - 1), n_recv.at[0])
+        weights_of(0, 1, BLOCK)
+    with jax.named_scope("arrive"):
+        landed(chunks(0, (far - 1) * (near - 1)), n_recv.at[1])
+    with jax.named_scope("group3"):
+        weights_of(1, far - 1, BLOCK)
 
     for s in range(steps):
         for d in reversed(range(1, n_cen)):
@@ -190,35 +222,46 @@
             with jax.named_scope("forward1"):
                 forward(s + 1)
             if s + 2 < steps:
-                send_own(s + 2)
+                send_far(s + 2)
         with jax.named_scope("stats" + str(s)):
             landed(stat.at[s, pl.ds(0, n_cen - 1)], s_recv.at[s])
         parts = stat[s]
         best = jnp.max(parts, axis=0)
         energy = best + jnp.log(jnp.sum(jnp.exp(parts - best[None]), axis=0))
-        scale = jnp.exp(tops[...] - energy)
+        whole[...] = energy
         for g in range(groups):
             en_ref[s:s + 1, g * LANES:(g + 1) * LANES] = energy[g:g + 1, :]
-        scale = jnp.concatenate([scale[g:g + 1, :] for g in range(groups)], axis=1)
+        energy = jnp.concatenate(
+            [whole[pl.ds(a_flip[d] * cols + j, 1), :] for d in range(far) for j in range(cols)], axis=1)
+
+        def scale_of(blk):
+            n = ROWS // BLOCK
+            rows = [block_top[blk * n + i, 0:1, :] if s == 0 else block_top[0, 0:1, :] for i in range(n)]
+            return [jnp.exp(row - energy) for row in rows]
+
+        def gather(blk):
+            rows = rows_of(blk)
+            weights = w_ref[rows, :]
+            resp = jnp.concatenate(
+                [weights[i * BLOCK:(i + 1) * BLOCK, :] * scale for i, scale in enumerate(scale_of(blk))], axis=0)
+            part = resp[:, :LANES]
+            for g in range(1, groups):
+                part = part + resp[:, g * LANES:(g + 1) * LANES]
+            count = jnp.sum(jnp.transpose(part), axis=0, keepdims=True)
+            sums = lax.dot_general(
+                resp.astype(jnp.bfloat16), x_ref[s], (((1,), (0,)), ((), ())),
+                preferred_element_type=jnp.float32)
+            got[s, p, blk, :ROWS, :] = sums
+            got[s, p, blk, ROWS:ROWS + 1, :] = count
+            for d in range(1, n_pts):
+                sums_copy(s, d, blk).start()
 
         with jax.named_scope("sums" + str(s)):
-            @pl.loop(0, n_blk)
-            def _(blk):
-                resp = w_ref[rows_of(blk), :] * scale
-                part = resp[:, :LANES]
-                for g in range(1, groups):
-                    part = part + resp[:, g * LANES:(g + 1) * LANES]
-                count = jnp.sum(jnp.transpose(part), axis=0, keepdims=True)
-                sums = lax.dot_general(
-                    resp.astype(jnp.bfloat16), x_ref[s], (((1,), (0,)), ((), ())),
-                    preferred_element_type=jnp.float32)
-                got[s, p, blk, :ROWS, :] = sums
-                got[s, p, blk, ROWS:ROWS + 1, :] = count
-                for d in range(1, n_pts):
-                    sums_copy(s, d, blk).start()
+            each(gather)
 
         if s + 1 < steps:
-            landed(chunks(s + 1, far * (near - 1)), near_sem(s + 1, 0))
+            with jax.named_scope("points" + str(s + 1)):
+                landed(chunks(s + 1, far * (near - 1)), n_recv.at[s + 2])
 
         def finish(blk, top):
             rows = rows_of(blk)
@@ -249,14 +292,14 @@
             return total + jnp.sum(weights, axis=0, keepdims=True)
 
         with jax.named_scope("finish" + str(s)):
-            top = lax.fori_loop(0, n_blk, finish, jnp.full((1, groups * LANES), -jnp.inf, jnp.float32))
+            top = folded(finish, jnp.full((1, groups * LANES), -jnp.inf, jnp.float32))
         if s + 1 < steps:
             with jax.named_scope("weigh"):
-                total = lax.fori_loop(0, n_blk, functools.partial(weigh, top), jnp.zeros_like(top))
-            part = top + jnp.log(total)
-            for g in range(groups):
-                tops[g:g + 1, :] = top[:, g * LANES:(g + 1) * LANES]
-                stat[s + 1, cen, g:g + 1, :] = part[:, g * LANES:(g + 1) * LANES]
+                total = folded(functools.partial(weigh, top), jnp.zeros_like(top))
+            block_top[0, 0:1, :] = top
+            for d in range(far):
+                lanes = slice(d * width, (d + 1) * width)
+                keep(s + 1, d, top[:, lanes], total[:, lanes])
 
     with jax.named_scope("drain"):
         for s in range(steps):
@@ -295,12 +338,13 @@
             pltpu.VMEM((k_loc, dim), jnp.float32),
             pltpu.VMEM((k_loc, dim), jnp.bfloat16),
             pltpu.VMEM((k_loc, LANES), jnp.float32),
+            pltpu.VMEM((k_loc // BLOCK, 8, batch), jnp.float32),
             pltpu.VMEM((groups, LANES), jnp.float32),
             pltpu.VMEM((steps, n_cen, groups, LANES), jnp.float32),
             pltpu.VMEM((steps, n_pts, n_blk, ROWS + 8, dim), jnp.float32),
             dma((steps,)),
             dma((far + steps - 1,)),
-            dma((far + steps - 1,)),
+            dma((steps + 1,)),
             dma((steps,)),
             dma((steps,)),
             dma((steps,)),

time: 30.4 us -> 29.8 us (0.980)
  Pallas kernels: 29.6 us -> 29 us
    pallas_call x1, Pallas kernels: 28.6 us -> 28 us  [on_device(): pl.pallas_call(functools.partial(kernel, far, near, n_pts), out_shape=(pl...]
where the time goes in v2:
time: 29.8 us; the launch traced here: 29.7 us
  Pallas kernels  29 us (97%)
  between operations  0.64 us (2%)
    pallas_call x1, Pallas kernels, on_device(): pl.pallas_call(functools.partial(kernel, far, near, n_pts), out_shape=(pl...  28 us
    pallas_call x1, Pallas kernels, on_device(): pl.pallas_call(emit, out_shape=(jax.ShapeDtypeStruct((k_loc, dim), jnp.fl...  0.99 us

profile of v2, /device:TPU:0, one launch (start us, length us, event | category | flops | bytes accessed | tf_op | source)
XLA Modules:
  0.0 29.7 jit_solution(1740738141591223547)
XLA Ops:
  0.6 28.0 %shard_map.41 = (f32[1024,256]{1,0:T(8,128)S(1)}, f32[2,512]{1,0:T(2,128)S(1)}) custom-call(bf16[2,32,256]{2,1,0:T(8,128)(2,1)} %pts_ref.1, f32[1024,256]{1,0:T(8,128)} %cen_ref.1), custom_call_target="tpu_custom_call" | custom-call | tf_op jit(solution)/shard_map/pallas_call | solution.py:329
  28.7 1.0 %shard_map.42 = (f32[1024,256]{1,0:T(8,128)}, f32[2,512]{1,0:T(2,128)}) custom-call(f32[1024,256]{1,0:T(8,128)S(1)} %get-tuple-element.4.value_ref, f32[2,512]{1,0:T(2,128)S(1)} %get-tuple-element.5.part_ref), custom_call_target="tpu_custom_call" | custom-call | tf_op jit(solution)/shard_map/pallas_call | solution.py:358

commit v3 on v2

--- a/solution.py
+++ b/solution.py
@@ -39,9 +39,12 @@
 
 
 def kernel(far, near, n_pts, pts_ref, cen_ref, out_ref, en_ref,
-           x_ref, w_ref, cur_ref, low_ref, sq_ref, block_top, whole, stat, got,
+           x_ref, w_ref, cur_ref, low_ref, sq_ref, block_top, whole, stat,
            p_send, f_recv, n_recv, s_send, s_recv, c_send, c_recv,
-           in_sem, cen_sem):
+           in_sem, cen_sem, *rest):
+    pair = n_pts == 2
+    acc_ref, part_ref = rest if pair else (None, None)
+    got = None if pair else rest[0]
     steps, own, dim = pts_ref.shape
     k_loc = cen_ref.shape[0]
     n_blk = k_loc // ROWS
@@ -92,7 +95,7 @@
         return pltpu.make_async_copy(cen_ref.at[rows, :], cur_ref.at[rows, :], cen_sem.at[blk])
 
     def chunk(s, d):
-        return x_ref.at[s, pl.ds(pl.multiple_of(d * width + b * own, own), own), :]
+        return x_ref.at[s, 0, pl.ds(pl.multiple_of(d * width + b * own, own), own), :]
 
     def pts_copy(s):
         return pltpu.make_async_copy(pts_ref.at[s], chunk(s, 0), in_sem.at[s])
@@ -108,7 +111,7 @@
             device_id={"cen": cen}, device_id_type=MESH).wait_send()
 
     def chunks(s, n):
-        return x_ref.at[s, pl.ds(0, n * own), :]
+        return x_ref.at[s, 0, pl.ds(0, n * own), :]
 
     def far_copy(s, d):
         return pltpu.make_async_remote_copy(
@@ -148,8 +151,13 @@
     def sums_copy(s, d, blk):
         return pltpu.make_async_remote_copy(
             src_ref=got.at[s, p, blk], dst_ref=got.at[s, p, blk],
-            send_sem=c_send.at[s], recv_sem=c_recv.at[s, blk],
+            send_sem=c_send.at[s], recv_sem=c_recv.at[s * n_blk + blk],
             device_id={"pts": pts_peers[d - 1]}, device_id_type=MESH)
+
+    def pair_copy(ref, i):
+        return pltpu.make_async_remote_copy(
+            src_ref=ref.at[0], dst_ref=ref.at[1], send_sem=c_send.at[i], recv_sem=c_recv.at[i],
+            device_id={"pts": pts_peers[0]}, device_id_type=MESH)
 
     for s in range(steps):
         pts_copy(s).start()
@@ -188,32 +196,74 @@
             lanes = slice(j * LANES, (j + 1) * LANES)
             stat[s, cen, pl.ds(a_flip[d] * cols + j, 1), :] = part[:, lanes]
 
-    def weights_of(d, n, size):
-        xs = x_ref[0, d * width:(d + n) * width, :]
+    def logits_of(low, sq, xs):
+        logits = lax.dot_general(
+            low, xs, (((1,), (1,)), ((), ())), preferred_element_type=jnp.float32)
+        if sq.shape[1] > 1:
+            sq = jnp.concatenate([sq] * (logits.shape[1] // LANES), axis=1)
+        return logits - sq
+
+    def weights_of(q, d, n):
+        lanes = slice(d * width, (d + n) * width)
+        xs = x_ref[0, q, lanes, :]
         pairs = []
-        for k in range(0, k_loc, size):
-            rows = slice(k, k + size)
-            logits = lax.dot_general(
-                low_ref[rows, :], xs, (((1,), (1,)), ((), ())),
-                preferred_element_type=jnp.float32)
-            logits = logits - jnp.concatenate([sq_ref[rows, :]] * (n * cols), axis=1)
+        for k in range(0, k_loc, BLOCK):
+            rows = slice(k, k + BLOCK)
+            logits = logits_of(low_ref[rows, :], sq_ref[rows, :], xs)
             top = jnp.max(logits, axis=0, keepdims=True)
             weights = jnp.exp(logits - top)
-            w_ref[rows, d * width:(d + n) * width] = weights
-            block_top[k // size, 0:1, d * width:(d + n) * width] = top
+            w_ref[q, rows, lanes] = weights
+            block_top[q, k // BLOCK, 0:1, lanes] = top
             pairs.append((top, jnp.sum(weights, axis=0, keepdims=True)))
-        top, total = combine(pairs)
+        return combine(pairs)
+
+    def first_weights(d, n):
+        top, total = weights_of(0, d, n)
         for i in range(n):
             lanes = slice(i * width, (i + 1) * width)
             keep(0, d + i, top[:, lanes], total[:, lanes])
 
+    def weigh(q, top, blk, total):
+        rows = rows_of(blk)
+        weights = jnp.exp(w_ref[q, rows, :] - top)
+        w_ref[q, rows, :] = weights
+        return total + jnp.sum(weights, axis=0, keepdims=True)
+
+    def resp_of(s, q, energy, blk):
+        rows = rows_of(blk)
+        weights = w_ref[q, rows, :]
+        if s > 0:
+            return weights * jnp.exp(block_top[q, 0, 0:1, :] - energy)
+        n = ROWS // BLOCK
+        return jnp.concatenate(
+            [weights[i * BLOCK:(i + 1) * BLOCK, :] * jnp.exp(block_top[q, blk * n + i, 0:1, :] - energy)
+             for i in range(n)], axis=0)
+
+    def lanes_of(resp):
+        part = resp[:, :LANES]
+        for g in range(1, groups):
+            part = part + resp[:, g * LANES:(g + 1) * LANES]
+        return part
+
+    def sums_of(s, q, resp):
+        return lax.dot_general(
+            resp.astype(jnp.bfloat16), x_ref[s, q], (((1,), (0,)), ((), ())),
+            preferred_element_type=jnp.float32)
+
+    def energy_of(s, q):
+        return jnp.concatenate(
+            [whole[s, q, pl.ds(a_flip[d] * cols + j, 1), :] for d in range(far) for j in range(cols)], axis=1)
+
+    lowest = jnp.full((1, groups * LANES), -jnp.inf, jnp.float32)
     with jax.named_scope("group0"):
         landed(chunks(0, near - 1), n_recv.at[0])
-        weights_of(0, 1, BLOCK)
+        first_weights(0, 1)
     with jax.named_scope("arrive"):
         landed(chunks(0, (far - 1) * (near - 1)), n_recv.at[1])
+        if pair:
+            pair_copy(x_ref.at[0], 0).start()
     with jax.named_scope("group3"):
-        weights_of(1, far - 1, BLOCK)
+        first_weights(1, far - 1)
 
     for s in range(steps):
         for d in reversed(range(1, n_cen)):
@@ -223,80 +273,107 @@
                 forward(s + 1)
             if s + 2 < steps:
                 send_far(s + 2)
+        if pair:
+            with jax.named_scope("other" + str(s)):
+                landed(x_ref.at[s, 1], c_recv.at[2 * s])
+                if s == 0:
+                    weights_of(1, 0, far)
+                else:
+                    def logits_block(blk, top):
+                        rows = rows_of(blk)
+                        logits = logits_of(low_ref[rows, :], sq_ref[rows, :], x_ref[s, 1])
+                        w_ref[1, rows, :] = logits
+                        return jnp.maximum(top, jnp.max(logits, axis=0, keepdims=True))
+
+                    top = folded(logits_block, lowest)
+                    folded(functools.partial(weigh, 1, top), jnp.zeros_like(top))
+                    block_top[1, 0, 0:1, :] = top
         with jax.named_scope("stats" + str(s)):
             landed(stat.at[s, pl.ds(0, n_cen - 1)], s_recv.at[s])
         parts = stat[s]
         best = jnp.max(parts, axis=0)
         energy = best + jnp.log(jnp.sum(jnp.exp(parts - best[None]), axis=0))
-        whole[...] = energy
+        whole[s, 0] = energy
+        if pair:
+            pair_copy(whole.at[s], 2 * s + 1).start()
         for g in range(groups):
             en_ref[s:s + 1, g * LANES:(g + 1) * LANES] = energy[g:g + 1, :]
-        energy = jnp.concatenate(
-            [whole[pl.ds(a_flip[d] * cols + j, 1), :] for d in range(far) for j in range(cols)], axis=1)
-
-        def scale_of(blk):
-            n = ROWS // BLOCK
-            rows = [block_top[blk * n + i, 0:1, :] if s == 0 else block_top[0, 0:1, :] for i in range(n)]
-            return [jnp.exp(row - energy) for row in rows]
-
-        def gather(blk):
+        energy = energy_of(s, 0)
+
+        def updated(blk, sums, column):
             rows = rows_of(blk)
-            weights = w_ref[rows, :]
-            resp = jnp.concatenate(
-                [weights[i * BLOCK:(i + 1) * BLOCK, :] * scale for i, scale in enumerate(scale_of(blk))], axis=0)
-            part = resp[:, :LANES]
-            for g in range(1, groups):
-                part = part + resp[:, g * LANES:(g + 1) * LANES]
-            count = jnp.sum(jnp.transpose(part), axis=0, keepdims=True)
-            sums = lax.dot_general(
-                resp.astype(jnp.bfloat16), x_ref[s], (((1,), (0,)), ((), ())),
-                preferred_element_type=jnp.float32)
-            got[s, p, blk, :ROWS, :] = sums
-            got[s, p, blk, ROWS:ROWS + 1, :] = count
-            for d in range(1, n_pts):
-                sums_copy(s, d, blk).start()
-
-        with jax.named_scope("sums" + str(s)):
-            each(gather)
-
-        if s + 1 < steps:
-            with jax.named_scope("points" + str(s + 1)):
-                landed(chunks(s + 1, far * (near - 1)), n_recv.at[s + 2])
-
-        def finish(blk, top):
-            rows = rows_of(blk)
-            landed(got.at[s, pl.ds(0, n_pts - 1), blk], c_recv.at[s, blk])
-            sums = got[s, 0, blk, :ROWS, :]
-            count = got[s, 0, blk, ROWS:ROWS + 1, :]
-            for i in range(1, n_pts):
-                sums = sums + got[s, i, blk, :ROWS, :]
-                count = count + got[s, i, blk, ROWS:ROWS + 1, :]
-            column = jnp.transpose(jnp.broadcast_to(1.0 / (1.0 + count), (LANES, ROWS)))
-            column = jnp.concatenate([column] * (dim // LANES), axis=1)
             value = (cur_ref[rows, :] + sums) * column
             if s + 1 == steps:
                 out_ref[rows, :] = value
-                return top
+                return None
             cur_ref[rows, :] = value
             low, sq = lowered(value)
-            logits = lax.dot_general(
-                low, x_ref[s + 1], (((1,), (1,)), ((), ())),
-                preferred_element_type=jnp.float32) - sq
-            w_ref[rows, :] = logits
-            return jnp.maximum(top, jnp.max(logits, axis=0, keepdims=True))
-
-        def weigh(top, blk, total):
-            rows = rows_of(blk)
-            weights = jnp.exp(w_ref[rows, :] - top)
-            w_ref[rows, :] = weights
-            return total + jnp.sum(weights, axis=0, keepdims=True)
+            if pair:
+                low_ref[rows, :] = low
+                sq_ref[rows, :] = jnp.broadcast_to(sq, (ROWS, LANES))
+            logits = logits_of(low, sq, x_ref[s + 1, 0])
+            w_ref[0, rows, :] = logits
+            return jnp.max(logits, axis=0, keepdims=True)
+
+        def arrived_next():
+            if s + 1 < steps:
+                with jax.named_scope("points" + str(s + 1)):
+                    landed(chunks(s + 1, far * (near - 1)), n_recv.at[s + 2])
+                    if pair:
+                        pair_copy(x_ref.at[s + 1], 2 * s + 2).start()
+
+        if pair:
+            def own_sums(blk):
+                rows = rows_of(blk)
+                resp = resp_of(s, 0, energy, blk)
+                part_ref[rows, :] = lanes_of(resp)
+                acc_ref[rows, :] = sums_of(s, 0, resp)
+
+            with jax.named_scope("sums" + str(s)):
+                each(own_sums)
+            arrived_next()
+            with jax.named_scope("whole" + str(s)):
+                landed(whole.at[s, 1], c_recv.at[2 * s + 1])
+            other = energy_of(s, 1)
+
+            def finish(blk, top):
+                rows = rows_of(blk)
+                resp = resp_of(s, 1, other, blk)
+                count = jnp.sum(part_ref[rows, :] + lanes_of(resp), axis=1, keepdims=True)
+                sums = acc_ref[rows, :] + sums_of(s, 1, resp)
+                best = updated(blk, sums, 1.0 / (1.0 + count))
+                return top if best is None else jnp.maximum(top, best)
+        else:
+            def gather(blk):
+                resp = resp_of(s, 0, energy, blk)
+                count = jnp.sum(jnp.transpose(lanes_of(resp)), axis=0, keepdims=True)
+                got[s, p, blk, :ROWS, :] = sums_of(s, 0, resp)
+                got[s, p, blk, ROWS:ROWS + 1, :] = count
+                for d in range(1, n_pts):
+                    sums_copy(s, d, blk).start()
+
+            with jax.named_scope("sums" + str(s)):
+                each(gather)
+            arrived_next()
+
+            def finish(blk, top):
+                if n_pts > 1:
+                    landed(got.at[s, pl.ds(0, n_pts - 1), blk], c_recv.at[s * n_blk + blk])
+                sums = got[s, 0, blk, :ROWS, :]
+                count = got[s, 0, blk, ROWS:ROWS + 1, :]
+                for i in range(1, n_pts):
+                    sums = sums + got[s, i, blk, :ROWS, :]
+                    count = count + got[s, i, blk, ROWS:ROWS + 1, :]
+                column = jnp.transpose(jnp.broadcast_to(1.0 / (1.0 + count), (LANES, ROWS)))
+                best = updated(blk, sums, jnp.concatenate([column] * (dim // LANES), axis=1))
+                return top if best is None else jnp.maximum(top, best)
 
         with jax.named_scope("finish" + str(s)):
-            top = folded(finish, jnp.full((1, groups * LANES), -jnp.inf, jnp.float32))
+            top = folded(finish, lowest)
         if s + 1 < steps:
             with jax.named_scope("weigh"):
-                total = folded(functools.partial(weigh, top), jnp.zeros_like(top))
-            block_top[0, 0:1, :] = top
+                total = folded(functools.partial(weigh, 0, top), jnp.zeros_like(top))
+            block_top[0, 0, 0:1, :] = top
             for d in range(far):
                 lanes = slice(d * width, (d + 1) * width)
                 keep(s + 1, d, top[:, lanes], total[:, lanes])
@@ -305,7 +382,11 @@
         for s in range(steps):
             sent(chunks(s, n_cen - 1), p_send.at[s])
             sent(stat.at[s, pl.ds(0, n_cen - 1)], s_send.at[s])
-            sent(got.at[s, pl.ds(0, n_pts - 1)], c_send.at[s])
+            if pair:
+                sent(x_ref.at[s, 0], c_send.at[2 * s])
+                sent(whole.at[s, 0], c_send.at[2 * s + 1])
+            elif n_pts > 1:
+                sent(got.at[s, pl.ds(0, n_pts - 1)], c_send.at[s])
 
 
 def emit(value_ref, part_ref, out_ref, en_ref, sems):
@@ -324,6 +405,7 @@
     n_cen = far * near
     batch = n_cen * own
     groups = batch // LANES
+    sides = 2 if n_pts == 2 else 1
     vmem = pl.BlockSpec(memory_space=pltpu.VMEM)
     dma = pltpu.SemaphoreType.DMA
     value, energy = pl.pallas_call(
@@ -333,25 +415,29 @@
         in_specs=[pl.BlockSpec(memory_space=pl.ANY)] * 2,
         out_specs=(vmem, vmem),
         scratch_shapes=[
-            pltpu.VMEM((steps, batch, dim), jnp.bfloat16),
-            pltpu.VMEM((k_loc, batch), jnp.float32),
+            pltpu.VMEM((steps, sides, batch, dim), jnp.bfloat16),
+            pltpu.VMEM((sides, k_loc, batch), jnp.float32),
             pltpu.VMEM((k_loc, dim), jnp.float32),
             pltpu.VMEM((k_loc, dim), jnp.bfloat16),
             pltpu.VMEM((k_loc, LANES), jnp.float32),
-            pltpu.VMEM((k_loc // BLOCK, 8, batch), jnp.float32),
-            pltpu.VMEM((groups, LANES), jnp.float32),
+            pltpu.VMEM((sides, k_loc // BLOCK, 8, batch), jnp.float32),
+            pltpu.VMEM((steps, sides, groups, LANES), jnp.float32),
             pltpu.VMEM((steps, n_cen, groups, LANES), jnp.float32),
-            pltpu.VMEM((steps, n_pts, n_blk, ROWS + 8, dim), jnp.float32),
             dma((steps,)),
             dma((far + steps - 1,)),
             dma((steps + 1,)),
             dma((steps,)),
             dma((steps,)),
-            dma((steps,)),
-            dma((steps, n_blk)),
+            dma((2 * steps,)),
+            dma((2 * steps if n_pts == 2 else steps * n_blk,)),
             dma((steps,)),
             dma((n_blk,)),
-        ],
+        ] + ([
+            pltpu.VMEM((k_loc, dim), jnp.float32),
+            pltpu.VMEM((k_loc, LANES), jnp.float32),
+        ] if n_pts == 2 else [
+            pltpu.VMEM((steps, n_pts, n_blk, ROWS + 8, dim), jnp.float32),
+        ]),
         compiler_params=pltpu.CompilerParams(
             collective_id=0, has_side_effects=True, vmem_limit_bytes=58 * 1024 * 1024),
     )(points, centroids)

time: 29.8 us -> 28 us (0.940)
  Pallas kernels: 29 us -> 27.2 us
    pallas_call x1, Pallas kernels: 28 us -> 26.2 us  [on_device(): pl.pallas_call(functools.partial(kernel, far, near, n_pts), out_shape=(pl...]
where the time goes in v3:
time: 28 us; the launch traced here: 27.8 us
  Pallas kernels  27.2 us (97%)
  between operations  0.64 us (2%)
    pallas_call x1, Pallas kernels, on_device(): pl.pallas_call(functools.partial(kernel, far, near, n_pts), out_shape=(pl...  26.2 us
    pallas_call x1, Pallas kernels, on_device(): pl.pallas_call(emit, out_shape=(jax.ShapeDtypeStruct((k_loc, dim), jnp.fl...  0.99 us

profile of v3, /device:TPU:0, one launch (start us, length us, event | category | flops | bytes accessed | tf_op | source)
XLA Modules:
  0.0 27.8 jit_solution(11653460416605436381)
XLA Ops:
  0.6 26.2 %shard_map.41 = (f32[1024,256]{1,0:T(8,128)S(1)}, f32[2,512]{1,0:T(2,128)S(1)}) custom-call(bf16[2,32,256]{2,1,0:T(8,128)(2,1)} %pts_ref.1, f32[1024,256]{1,0:T(8,128)} %cen_ref.1), custom_call_target="tpu_custom_call" | custom-call | tf_op jit(solution)/shard_map/pallas_call | solution.py:411
  26.8 1.0 %shard_map.42 = (f32[1024,256]{1,0:T(8,128)}, f32[2,512]{1,0:T(2,128)}) custom-call(f32[1024,256]{1,0:T(8,128)S(1)} %get-tuple-element.4.value_ref, f32[2,512]{1,0:T(2,128)S(1)} %get-tuple-element.5.part_ref), custom_call_target="tpu_custom_call" | custom-call | tf_op jit(solution)/shard_map/pallas_call | solution.py:444

commit v4 on v3

--- a/solution.py
+++ b/solution.py
@@ -26,7 +26,7 @@
 def flips(i, n):
     steps, bit = [], 1
     while bit < n:
-        steps.append((bit, bit - 2 * bit * lax.rem(i // bit, 2)))
+        steps.append((bit, bit - 2 * bit * lax.rem(lax.div(i, bit), 2)))
         bit *= 2
     peers = []
     for d in range(n):
@@ -55,7 +55,7 @@
     unroll = groups * n_blk <= UNROLL
     cen = lax.axis_index("cen")
     p = lax.axis_index("pts")
-    a = cen // near
+    a = lax.div(cen, near)
     b = lax.rem(cen, near)
     a_flip = flips(a, far)
     b_flip = flips(b, near)
@@ -115,13 +115,13 @@
 
     def far_copy(s, d):
         return pltpu.make_async_remote_copy(
-            src_ref=pts_ref.at[s], dst_ref=chunk(s, d),
+            src_ref=chunk(s, 0), dst_ref=chunk(s, d),
             send_sem=p_send.at[s], recv_sem=f_recv.at[d if s == 0 else far + s - 1],
             device_id={"cen": a_flip[d] * near + b}, device_id_type=MESH)
 
     def near_copy(s, d, e):
         return pltpu.make_async_remote_copy(
-            src_ref=pts_ref.at[s] if d == 0 else chunk(s, d), dst_ref=chunk(s, d),
+            src_ref=chunk(s, d), dst_ref=chunk(s, d),
             send_sem=p_send.at[s], recv_sem=n_recv.at[min(d, 1) if s == 0 else s + 1],
             device_id={"cen": a * near + b_flip[e]}, device_id_type=MESH)
 
@@ -148,6 +148,21 @@
             send_sem=s_send.at[s], recv_sem=s_recv.at[s],
             device_id={"cen": a_flip[d // near] * near + b_flip[d % near]}, device_id_type=MESH)
 
+    def cross_copy(s, d):
+        return pltpu.make_async_remote_copy(
+            src_ref=stat.at[s, cen], dst_ref=stat.at[s, n_cen + cen],
+            send_sem=s_send.at[s], recv_sem=s_recv.at[steps + s],
+            device_id={"cen": a_flip[d // near] * near + b_flip[d % near], "pts": pts_peers[0]},
+            device_id_type=MESH)
+
+    def crossed(s):
+        return pair and s > 0
+
+    def total_of(s, q):
+        parts = stat[s, q * n_cen:(q + 1) * n_cen]
+        best = jnp.max(parts, axis=0)
+        return best + jnp.log(jnp.sum(jnp.exp(parts - best[None]), axis=0))
+
     def sums_copy(s, d, blk):
         return pltpu.make_async_remote_copy(
             src_ref=got.at[s, p, blk], dst_ref=got.at[s, p, blk],
@@ -166,6 +181,9 @@
     def _(blk):
         cen_copy(blk).start()
 
+    with jax.named_scope("own"):
+        for s in range(steps):
+            pts_copy(s).wait()
     with jax.named_scope("entry"):
         pl.semaphore_wait(barrier, (far - 1) + (near - 1) + (n_pts - 1))
         send_far(0)
@@ -183,8 +201,6 @@
         forward(0)
     if steps > 1:
         send_far(1)
-    for s in range(steps):
-        pts_copy(s).wait()
 
     def combine(pairs):
         best = functools.reduce(jnp.maximum, [top for top, _ in pairs])
@@ -268,6 +284,9 @@
     for s in range(steps):
         for d in reversed(range(1, n_cen)):
             stat_copy(s, d).start()
+        if crossed(s):
+            for d in reversed(range(n_cen)):
+                cross_copy(s, d).start()
         if s + 1 < steps:
             with jax.named_scope("forward1"):
                 forward(s + 1)
@@ -290,11 +309,9 @@
                     block_top[1, 0, 0:1, :] = top
         with jax.named_scope("stats" + str(s)):
             landed(stat.at[s, pl.ds(0, n_cen - 1)], s_recv.at[s])
-        parts = stat[s]
-        best = jnp.max(parts, axis=0)
-        energy = best + jnp.log(jnp.sum(jnp.exp(parts - best[None]), axis=0))
+        energy = total_of(s, 0)
         whole[s, 0] = energy
-        if pair:
+        if pair and not crossed(s):
             pair_copy(whole.at[s], 2 * s + 1).start()
         for g in range(groups):
             en_ref[s:s + 1, g * LANES:(g + 1) * LANES] = energy[g:g + 1, :]
@@ -333,15 +350,33 @@
                 each(own_sums)
             arrived_next()
             with jax.named_scope("whole" + str(s)):
-                landed(whole.at[s, 1], c_recv.at[2 * s + 1])
+                if crossed(s):
+                    landed(stat.at[s, pl.ds(0, n_cen)], s_recv.at[steps + s])
+                    whole[s, 1] = total_of(s, 1)
+                else:
+                    landed(whole.at[s, 1], c_recv.at[2 * s + 1])
             other = energy_of(s, 1)
 
-            def finish(blk, top):
+            def other_sums(blk):
                 rows = rows_of(blk)
                 resp = resp_of(s, 1, other, blk)
                 count = jnp.sum(part_ref[rows, :] + lanes_of(resp), axis=1, keepdims=True)
-                sums = acc_ref[rows, :] + sums_of(s, 1, resp)
-                best = updated(blk, sums, 1.0 / (1.0 + count))
+                part_ref[rows, :] = jnp.broadcast_to(1.0 / (1.0 + count), (ROWS, LANES))
+                acc_ref[rows, :] = acc_ref[rows, :] + sums_of(s, 1, resp)
+
+            if s + 1 < steps:
+                with jax.named_scope("othersums" + str(s)):
+                    each(other_sums)
+
+            def finish(blk, top):
+                rows = rows_of(blk)
+                if s + 1 == steps:
+                    resp = resp_of(s, 1, other, blk)
+                    count = jnp.sum(part_ref[rows, :] + lanes_of(resp), axis=1, keepdims=True)
+                    updated(blk, acc_ref[rows, :] + sums_of(s, 1, resp), 1.0 / (1.0 + count))
+                    return top
+                column = jnp.concatenate([part_ref[rows, :]] * (dim // LANES), axis=1)
+                best = updated(blk, acc_ref[rows, :], column)
                 return top if best is None else jnp.maximum(top, best)
         else:
             def gather(blk):
@@ -381,10 +416,11 @@
     with jax.named_scope("drain"):
         for s in range(steps):
             sent(chunks(s, n_cen - 1), p_send.at[s])
-            sent(stat.at[s, pl.ds(0, n_cen - 1)], s_send.at[s])
+            sent(stat.at[s, pl.ds(0, (2 * n_cen if crossed(s) else n_cen) - 1)], s_send.at[s])
             if pair:
                 sent(x_ref.at[s, 0], c_send.at[2 * s])
-                sent(whole.at[s, 0], c_send.at[2 * s + 1])
+                if not crossed(s):
+                    sent(whole.at[s, 0], c_send.at[2 * s + 1])
             elif n_pts > 1:
                 sent(got.at[s, pl.ds(0, n_pts - 1)], c_send.at[s])
 
@@ -422,12 +458,12 @@
             pltpu.VMEM((k_loc, LANES), jnp.float32),
             pltpu.VMEM((sides, k_loc // BLOCK, 8, batch), jnp.float32),
             pltpu.VMEM((steps, sides, groups, LANES), jnp.float32),
-            pltpu.VMEM((steps, n_cen, groups, LANES), jnp.float32),
+            pltpu.VMEM((steps, sides * n_cen, groups, LANES), jnp.float32),
             dma((steps,)),
             dma((far + steps - 1,)),
             dma((steps + 1,)),
             dma((steps,)),
-            dma((steps,)),
+            dma((sides * steps,)),
             dma((2 * steps,)),
             dma((2 * steps if n_pts == 2 else steps * n_blk,)),
             dma((steps,)),

time: 28 us -> 27 us (0.964)
  Pallas kernels: 27.2 us -> 26.1 us
    pallas_call x1, Pallas kernels: 26.2 us -> 25.1 us  [on_device(): pl.pallas_call(functools.partial(kernel, far, near, n_pts), out_shape=(pl...]
where the time goes in v4:
time: 27 us; the launch traced here: 26.8 us
  Pallas kernels  26.1 us (97%)
  between operations  0.64 us (2%)
    pallas_call x1, Pallas kernels, on_device(): pl.pallas_call(functools.partial(kernel, far, near, n_pts), out_shape=(pl...  25.1 us
    pallas_call x1, Pallas kernels, on_device(): pl.pallas_call(emit, out_shape=(jax.ShapeDtypeStruct((k_loc, dim), jnp.fl...  0.99 us

profile of v4, /device:TPU:0, one launch (start us, length us, event | category | flops | bytes accessed | tf_op | source)
XLA Modules:
  0.0 26.8 jit_solution(15713852573116865033)
XLA Ops:
  0.6 25.1 %shard_map.41 = (f32[1024,256]{1,0:T(8,128)S(1)}, f32[2,512]{1,0:T(2,128)S(1)}) custom-call(bf16[2,32,256]{2,1,0:T(8,128)(2,1)} %pts_ref.1, f32[1024,256]{1,0:T(8,128)} %cen_ref.1), custom_call_target="tpu_custom_call" | custom-call | tf_op jit(solution)/shard_map/pallas_call | solution.py:447
  25.8 1.0 %shard_map.42 = (f32[1024,256]{1,0:T(8,128)}, f32[2,512]{1,0:T(2,128)}) custom-call(f32[1024,256]{1,0:T(8,128)S(1)} %get-tuple-element.4.value_ref, f32[2,512]{1,0:T(2,128)S(1)} %get-tuple-element.5.part_ref), custom_call_target="tpu_custom_call" | custom-call | tf_op jit(solution)/shard_map/pallas_call | solution.py:480

commit v5 on v4

--- a/solution.py
+++ b/solution.py
@@ -13,6 +13,7 @@
 ROWS = 256
 BLOCK = 128
 UNROLL = 32
+HUB = 1
 
 
 def split(n):
@@ -43,7 +44,7 @@
            p_send, f_recv, n_recv, s_send, s_recv, c_send, c_recv,
            in_sem, cen_sem, *rest):
     pair = n_pts == 2
-    acc_ref, part_ref = rest if pair else (None, None)
+    acc_ref, part_ref, hub_ref, h_send = rest if pair else (None,) * 4
     got = None if pair else rest[0]
     steps, own, dim = pts_ref.shape
     k_loc = cen_ref.shape[0]
@@ -68,6 +69,18 @@
         pl.semaphore_signal(barrier, inc=1, device_id={"cen": a * near + peer}, device_id_type=MESH)
     for peer in pts_peers:
         pl.semaphore_signal(barrier, inc=1, device_id={"pts": peer}, device_id_type=MESH)
+    if pair:
+        @pl.when(p == HUB)
+        def _():
+            for peer in a_flip[1:]:
+                pl.semaphore_signal(
+                    barrier, inc=1, device_id={"cen": peer * near + b, "pts": 1 - HUB}, device_id_type=MESH)
+
+        @pl.when(p != HUB)
+        def _():
+            for peer in b_flip[1:]:
+                pl.semaphore_signal(
+                    barrier, inc=1, device_id={"cen": a * near + peer, "pts": HUB}, device_id_type=MESH)
 
     def rows_of(blk):
         return pl.ds(blk * ROWS if isinstance(blk, int) else pl.multiple_of(blk * ROWS, ROWS), ROWS)
@@ -124,6 +137,24 @@
             src_ref=chunk(s, d), dst_ref=chunk(s, d),
             send_sem=p_send.at[s], recv_sem=n_recv.at[min(d, 1) if s == 0 else s + 1],
             device_id={"cen": a * near + b_flip[e]}, device_id_type=MESH)
+
+    def hub_copy(d):
+        return pltpu.make_async_remote_copy(
+            src_ref=chunk(0, 0), dst_ref=hub_ref.at[d],
+            send_sem=p_send.at[0], recv_sem=f_recv.at[far + steps - 1 + d],
+            device_id={"cen": a_flip[d] * near + b, "pts": HUB}, device_id_type=MESH)
+
+    def relay_copy(d, e):
+        return pltpu.make_async_remote_copy(
+            src_ref=hub_ref.at[d], dst_ref=chunk(0, d),
+            send_sem=h_send.at[0], recv_sem=n_recv.at[1],
+            device_id={"cen": a * near + b_flip[e], "pts": 1 - HUB}, device_id_type=MESH)
+
+    def relay():
+        for d in range(1, far):
+            landed(hub_ref.at[d], f_recv.at[far + steps - 1 + d])
+            for e in reversed(range(near)):
+                relay_copy(d, e).start()
 
     def send_near(s, d):
         for e in reversed(range(1, near)):
@@ -185,8 +216,19 @@
         for s in range(steps):
             pts_copy(s).wait()
     with jax.named_scope("entry"):
-        pl.semaphore_wait(barrier, (far - 1) + (near - 1) + (n_pts - 1))
-        send_far(0)
+        extra = jnp.where(p == HUB, near - 1, far - 1) if pair else 0
+        pl.semaphore_wait(barrier, (far - 1) + (near - 1) + (n_pts - 1) + extra)
+        if pair:
+            @pl.when(p == HUB)
+            def _():
+                send_far(0)
+
+            @pl.when(p != HUB)
+            def _():
+                for d in reversed(range(1, far)):
+                    hub_copy(d).start()
+        else:
+            send_far(0)
         send_near(0, 0)
 
     with jax.named_scope("prepare"):
@@ -198,7 +240,13 @@
             sq_ref[rows, :] = jnp.broadcast_to(sq, (ROWS, LANES))
 
     with jax.named_scope("forward0"):
-        forward(0)
+        if pair:
+            @pl.when(p == HUB)
+            def _():
+                forward(0)
+                relay()
+        else:
+            forward(0)
     if steps > 1:
         send_far(1)
 
@@ -275,7 +323,16 @@
         landed(chunks(0, near - 1), n_recv.at[0])
         first_weights(0, 1)
     with jax.named_scope("arrive"):
-        landed(chunks(0, (far - 1) * (near - 1)), n_recv.at[1])
+        if pair:
+            @pl.when(p == HUB)
+            def _():
+                landed(chunks(0, (far - 1) * (near - 1)), n_recv.at[1])
+
+            @pl.when(p != HUB)
+            def _():
+                landed(chunks(0, (far - 1) * near), n_recv.at[1])
+        else:
+            landed(chunks(0, (far - 1) * (near - 1)), n_recv.at[1])
         if pair:
             pair_copy(x_ref.at[0], 0).start()
     with jax.named_scope("group3"):
@@ -415,7 +472,17 @@
 
     with jax.named_scope("drain"):
         for s in range(steps):
-            sent(chunks(s, n_cen - 1), p_send.at[s])
+            if pair and s == 0:
+                @pl.when(p == HUB)
+                def _():
+                    sent(chunks(0, n_cen - 1), p_send.at[0])
+                    sent(chunks(0, (far - 1) * near), h_send.at[0])
+
+                @pl.when(p != HUB)
+                def _():
+                    sent(chunks(0, far + near - 2), p_send.at[0])
+            else:
+                sent(chunks(s, n_cen - 1), p_send.at[s])
             sent(stat.at[s, pl.ds(0, (2 * n_cen if crossed(s) else n_cen) - 1)], s_send.at[s])
             if pair:
                 sent(x_ref.at[s, 0], c_send.at[2 * s])
@@ -460,7 +527,7 @@
             pltpu.VMEM((steps, sides, groups, LANES), jnp.float32),
             pltpu.VMEM((steps, sides * n_cen, groups, LANES), jnp.float32),
             dma((steps,)),
-            dma((far + steps - 1,)),
+            dma((2 * far + steps - 1,)),
             dma((steps + 1,)),
             dma((steps,)),
             dma((sides * steps,)),
@@ -471,6 +538,8 @@
         ] + ([
             pltpu.VMEM((k_loc, dim), jnp.float32),
             pltpu.VMEM((k_loc, LANES), jnp.float32),
+            pltpu.VMEM((far, own, dim), jnp.bfloat16),
+            dma((1,)),
         ] if n_pts == 2 else [
             pltpu.VMEM((steps, n_pts, n_blk, ROWS + 8, dim), jnp.float32),
         ]),

time: 27 us -> 26.4 us (0.978)
  Pallas kernels: 26.1 us -> 25.6 us
    pallas_call x1, Pallas kernels: 25.1 us -> 24.6 us  [on_device(): pl.pallas_call(functools.partial(kernel, far, near, n_pts), out_shape=(pl...]
where the time goes in v5:
time: 26.4 us; the launch traced here: 26.2 us
  Pallas kernels  25.6 us (97%)
  between operations  0.64 us (2%)
    pallas_call x1, Pallas kernels, on_device(): pl.pallas_call(functools.partial(kernel, far, near, n_pts), out_shape=(pl...  24.6 us
    pallas_call x1, Pallas kernels, on_device(): pl.pallas_call(emit, out_shape=(jax.ShapeDtypeStruct((k_loc, dim), jnp.fl...  0.99 us

profile of v5, /device:TPU:0, one launch (start us, length us, event | category | flops | bytes accessed | tf_op | source)
XLA Modules:
  0.0 26.2 jit_solution(4603764320180295583)
XLA Ops:
  0.6 24.6 %shard_map.41 = (f32[1024,256]{1,0:T(8,128)S(1)}, f32[2,512]{1,0:T(2,128)S(1)}) custom-call(bf16[2,32,256]{2,1,0:T(8,128)(2,1)} %pts_ref.1, f32[1024,256]{1,0:T(8,128)} %cen_ref.1), custom_call_target="tpu_custom_call" | custom-call | tf_op jit(solution)/shard_map/pallas_call | solution.py:514
  25.2 1.0 %shard_map.42 = (f32[1024,256]{1,0:T(8,128)}, f32[2,512]{1,0:T(2,128)}) custom-call(f32[1024,256]{1,0:T(8,128)S(1)} %get-tuple-element.4.value_ref, f32[2,512]{1,0:T(2,128)S(1)} %get-tuple-element.5.part_ref), custom_call_target="tpu_custom_call" | custom-call | tf_op jit(solution)/shard_map/pallas_call | solution.py:549
